TPU v7x, 128 devices: a whole 4x4x4 slice. The times are simulated.
128 devices in a mesh: member: 2 (over x_lo), dp: 64 (over y, x_hi, z, core).
Axes of the slice: x: 4 (x_hi: 2, x_lo: 2; x = x_hi * 2 + x_lo), y: 4, z: 4, core: 2. Of those that a mesh axis runs over, the one named last changes fastest.
Arguments:
- features: bfloat16 [256, 256, 1024], P(('dp', 'member')), may hold values from -10 to 10
- teacher_logits: bfloat16 [4, 256, 256, 256], P('member', 'dp'), may hold values from -320 to 320
- lengths: int32 [256], P(('dp', 'member')), may hold values from 16 to 256
- gain_conv: float32 [1024], replicated, may hold values from 0.5 to 1.5
- weight_in: bfloat16 [1024, 2048], replicated, may hold values from -0.1875 to 0.1875
- weight_depth: float32 [31, 1024], replicated, may hold values from -1 to 1
- weight_out: bfloat16 [1024, 1024], replicated, may hold values from -0.1875 to 0.1875
- gain_out: float32 [1024], replicated, may hold values from 0.5 to 1.5
- head_weight: bfloat16 [1024, 256], replicated, may hold values from -1 to 1
Outputs:
- grad_gain_conv: float32 [1024], replicated
- grad_weight_in: float32 [1024, 2048], replicated
- grad_weight_depth: float32 [31, 1024], replicated
- grad_weight_out: float32 [1024, 1024], replicated
- grad_gain_out: float32 [1024], replicated
- grad_head: float32 [1024, 256], replicated
- utt_loss: float32 [256], P(('dp', 'member'))
All inputs are finite; a program needn't handle non-finite values.
Results may differ from a plain program's by a relative error of at most 0.015.
Values may be sent and summed in bfloat16 or wider, within the bound.
A program may use at most 128 MiB of HBM per device.

v0:
```python
import jax
import jax.numpy as jnp
from jax import lax
from jax.sharding import PartitionSpec as P

TEACHERS = 4


def normalize(values, gain):
    average = jnp.mean(values, axis=-1, keepdims=True)
    centred = values - average
    spread = jnp.mean(centred * centred, axis=-1, keepdims=True)
    return centred * lax.rsqrt(spread + 1e-05) * gain


def live_frames(lengths, frames):
    return (jnp.arange(frames, dtype=jnp.int32)[None, :] < lengths[:, None]).astype(jnp.float32)


def lower_part(conv_weights, features, lengths):
    gain_conv, weight_in, weight_depth, weight_out = conv_weights
    utterances, frames, model_width = features.shape
    widened = features.astype(jnp.float32)
    normed = (
        normalize(widened, gain_conv).astype(jnp.bfloat16).reshape(utterances * frames, model_width)
    )
    projected = jnp.dot(normed, weight_in, preferred_element_type=jnp.float32)
    live_mask = live_frames(lengths, frames)
    gated = (projected[:, :model_width] * jax.nn.sigmoid(projected[:, model_width:])).reshape(
        utterances, frames, model_width
    ) * live_mask[:, :, None]
    half_width = weight_depth.shape[0] // 2
    convolved = lax.conv_general_dilated(
        gated,
        weight_depth[:, None, :],
        (1,),
        [(half_width, half_width)],
        dimension_numbers=("NWC", "WIO", "NWC"),
        feature_group_count=model_width,
        precision=lax.Precision.HIGHEST,
    )
    activated = (
        (convolved * jax.nn.sigmoid(convolved))
        .astype(jnp.bfloat16)
        .reshape(utterances * frames, model_width)
    )
    update = jnp.dot(activated, weight_out, preferred_element_type=jnp.float32)
    return widened + update.reshape(utterances, frames, model_width)


def upper_part(top_weights, residual_sum, target, lengths, mean_frames):
    gain_out, head_weight = top_weights
    utterances, frames, model_width = residual_sum.shape
    final_norm = (
        normalize(residual_sum, gain_out)
        .astype(jnp.bfloat16)
        .reshape(utterances * frames, model_width)
    )
    student_logits = jnp.dot(final_norm, head_weight, preferred_element_type=jnp.float32)
    student_logp = jax.nn.log_softmax(student_logits, axis=-1).reshape(utterances, frames, -1)
    cross_entropy = -jnp.sum(target * student_logp, axis=-1)
    return jnp.sum(cross_entropy * live_frames(lengths, frames), axis=-1) / mean_frames


def student_losses(weights, features, target, lengths, mean_frames):
    residual_sum = lower_part(weights[:4], features, lengths)
    return upper_part(weights[4:], residual_sum, target, lengths, mean_frames)


def teacher_target(summed):
    return jnp.exp(jax.nn.log_softmax(summed / TEACHERS, axis=-1))


def on_device(
    features,
    teacher_logits,
    lengths,
    gain_conv,
    weight_in,
    weight_depth,
    weight_out,
    gain_out,
    head_weight,
):
    frame_total = lax.psum(jnp.sum(lengths.astype(jnp.float32)), ("member", "dp"))
    own_count = lengths.shape[0]
    mean_frames = frame_total / (own_count * lax.axis_size("member") * lax.axis_size("dp"))
    local_sum = jnp.sum(jax.nn.log_softmax(teacher_logits.astype(jnp.float32), axis=-1), axis=0)
    group_sum = lax.psum(local_sum, "member")
    own_sum = lax.dynamic_slice_in_dim(
        group_sum, lax.axis_index("member") * own_count, own_count, 0
    )
    target = teacher_target(own_sum)
    weights = (gain_conv, weight_in, weight_depth, weight_out, gain_out, head_weight)

    def local_loss(trainable):
        return student_losses(trainable, features, target, lengths, mean_frames)

    losses, pullback = jax.vjp(local_loss, weights)
    gradients = pullback(jnp.ones_like(losses))[0]
    totals = lax.psum(
        (
            gradients[0],
            gradients[1].astype(jnp.float32),
            gradients[2],
            gradients[3].astype(jnp.float32),
            gradients[4],
            gradients[5].astype(jnp.float32),
        ),
        ("member", "dp"),
    )
    return (totals[0], totals[1], totals[2], totals[3], totals[4], totals[5], losses)


def solution(mesh):
    in_specs = (
        P(("dp", "member"), None, None),
        P("member", "dp", None, None),
        P(("dp", "member")),
        P(),
        P(),
        P(),
        P(),
        P(),
        P(),
    )
    out_specs = (P(), P(), P(), P(), P(), P(), P(("dp", "member")))
    return jax.shard_map(
        on_device, mesh=mesh, in_specs=in_specs, out_specs=out_specs, check_vma=False
    )
```

profile of v0, /device:TPU:1, one launch (start us, length us, event | category | flops | bytes accessed | tf_op | source)
XLA Modules:
  0.0 415.8 jit_solution(1241103938338909669)
XLA Ops:
  8.9 14.1 %fusion.27 = f32[4,256,256]{2,1,0:T(8,128)} fusion(bf16[2,4,256,256]{3,2,1,0:T(8,128)(2,1)} %param.10, f32[2,4,256]{2,1,0:T(4,128)S(1)} %reduce_max.36), kind=kOutput, calls=%fused_computation.43 | output fusion | flops 2885887 | bytes 2105344 | tf_op jit(solution)/shard_map/jit(log_softmax)/reduce_sum | solution.py:88
  23.7 69.0 %psum.57 = f32[]{:T(128)} all-reduce(f32[]{:T(128)} %convert_reduce_fusion.1), channel_id=1, replica_groups=mesh['member'=2,'dp'=64] {'member','dp'}, use_global_device_ids=true, to_apply=%region_9.10 | all-reduce | flops 1 | bytes 8 | tf_op jit(solution)/shard_map/psum | solution.py:85
  95.2 2.4 fusion.73
  101.2 1.6 copy.69
  104.2 1.9 fusion.3
  106.1 11.0 %multiply_convert_fusion = (bf16[16,36,1024]{2,0,1:T(8,128)(2,1)S(1)}, f32[16,36,1024]{2,0,1:T(8,128)}, f32[16,36,1024]{2,0,1:T(8,128)}, f32[16,36,1024]{2,0,1:T(8,128)}) fusion(f32[31,1,1024]{2,0,1:T(8,128)S(1)} %bitcast.83, f32[2,8,66,1024]{3,0,2,1:T(2,128)S(1)} %fusion.3, pred[16,36]{0,1:T(8,128)(4,1)S(1)} %copy-done.32), kind=kOutput, calls=%fused_computation.32 | convolution fusion | flops 224133120 | bytes 12710464 | tf_op jit(solution)/shard_map/jvp()/conv_general_dilated | solution.py:33
  117.2 1.7 copy.49
  118.9 2.7 reshape.152
  121.6 2.6 fusion.71
  128.1 2.9 copy.56
  130.9 2.9 reshape.165
  133.8 1.7 copy-done.20
  135.5 2.9 copy.50
  138.3 2.9 reshape.161
  141.2 1.7 copy-done.19
  142.9 2.9 copy.53
  145.7 3.0 reshape.163
  149.5 2.0 subtract_subtract_fusion
  152.8 2.1 fusion.70
  162.7 9.6 %fusion.31 = f32[2,256,1024]{2,0,1:T(2,128)S(1)} fusion(f32[2,256,1024]{2,1,0:T(8,128)S(1)} %slice-done, f32[2,256,1024]{2,1,0:T(8,128)S(1)} %slice-done.2, f32[2,256,1024]{2,1,0:T(8,128)S(1)} %slice-done.1, f32[2,256,1024]{2,1,0:T(8,128)S(1)} %convert.9), kind=kLoop, calls=%fused_computation.50 | loop fusion | flops 2097152 | bytes 10485760 | tf_op jit(solution)/shard_map/transpose(jvp())/add_any | solution.py:43
  172.2 27.8 %fusion.68 = f32[31,1,1024]{2,1,0:T(1,128)S(1)} fusion(f32[2,256,1024]{2,0,1:T(2,128)S(1)} %fusion.31, f32[2,256,1024]{2,1,0:T(8,128)S(1)} %copy-done.12), kind=kOutput, calls=%fused_computation.115 | convolution fusion | flops 189136896 | bytes 4321280 | tf_op jit(solution)/shard_map/transpose(jvp())/conv_general_dilated | solution.py:33
  201.3 3.3 fusion.35
  206.9 5.5 %fusion.39 = f32[16,36,1024]{2,0,1:T(8,128)S(1)} fusion(f32[2,7,30,1024]{3,1,0,2:T(8,128)S(1)} %slice.22, f32[2,8,36,1024]{3,1,0,2:T(8,128)S(1)} %copy.59, pred[16,36]{0,1:T(8,128)(4,1)S(1)} %copy-done.32, f32[31,1024,1]{1,0,2:T(8,128)S(1)} %bitcast.84), kind=kOutput, calls=%fused_computation.67 | convolution fusion | flops 223248384 | bytes 6566464 | tf_op jit(solution)/shard_map/transpose(jvp())/conv_general_dilated | solution.py:33
  212.3 2.9 copy.61
  215.2 3.1 reshape.159
  218.3 1.9 slice_multiply_fusion
  222.3 5.8 %convert_convert_fusion = f32[1024,2048]{1,0:T(8,128)} fusion(bf16[512,1024]{1,0:T(8,128)(2,1)S(1)} %bitcast.80, f32[512,1024]{1,0:T(8,128)S(1)} %get-tuple-element.18, f32[512,1024]{1,0:T(8,128)S(1)} %get-tuple-element.17), kind=kOutput, calls=%fused_computation.15 | convolution fusion | flops 2152726528 | bytes 13631488 | tf_op jit(solution)/shard_map/transpose(jvp())/dot_general | solution.py:27
  229.7 5.2 %fusion.22 = f32[1024]{0:T(1024)S(1)} fusion(bf16[2,256,1024]{2,1,0:T(8,128)(2,1)S(1)} %copy-done.6, f32[2,256]{1,0:T(2,128)S(1)} %add_rsqrt_fusion, f32[2,256]{1,0:T(2,128)S(1)} %broadcast_multiply_fusion.3, bf16[1024,2048]{1,0:T(8,128)(2,1)} %param.13, f32[512,1024]{1,0:T(8,128)} %copy-done.15, f32[512,1024]{1,0:T(8,128)S(1)} %copy-done.14), kind=kOutput, calls=%fused_computation.37 | convolution fusion | flops 2152201216 | bytes 9445376 | tf_op jit(solution)/shard_map/transpose(jvp())/dot_general | solution.py:27
  234.9 63.3 %all-reduce.2 = (f32[1024]{0:T(1024)}, f32[1024]{0:T(1024)}) all-reduce(f32[1024]{0:T(1024)S(1)} %fusion.22, f32[1024]{0:T(1024)S(1)} %get-tuple-element.7), channel_id=1, replica_groups=mesh['member'=2,'dp'=64] {'member','dp'}, use_global_device_ids=true, to_apply=%region_18.19 | all-reduce | flops 2048 | bytes 16384 | tf_op jit(solution)/shard_map/psum | solution.py:101
  299.0 97.3 %all-reduce.9.cloned.1.call-done = (f32[1024,2048]{1,0:T(8,128)}, f32[31,1024]{1,0:T(8,128)}, f32[1024,1024]{1,0:T(8,128)}, f32[1024,256]{1,0:T(8,128)}) async-done(((f32[1024,2048]{1,0:T(8,128)}, f32[31,1024]{1,0:T(8,128)}, f32[1024,1024]{1,0:T(8,128)}, f32[1024,256]{1,0:T(8,128)}), (f32[1024,2048]{1,0:T(8,128)}, f32[31,1024]{1,0:T(8,128)}, f32[1024,1024]{1,0:T(8,128)}, ...) | async-done | bytes 13758480 | tf_op jit(solution)/shard_map/psum | solution.py:101
  396.3 8.0 %copy.104 = f32[1024,2048]{1,0:T(8,128)} copy(f32[1024,2048]{1,0:T(8,128)} %get-tuple-element.29) | data formatting | bytes 16777216
  405.0 2.1 copy.106
  (119 shorter events, 32.9 us)
Async XLA Ops:
  7.2 114.4 %copy-start = (bf16[1024,1024]{1,0:T(8,128)(2,1)S(1)}, bf16[1024,1024]{1,0:T(8,128)(2,1)}, u32[]{:S(2)}) copy-start(bf16[1024,1024]{1,0:T(8,128)(2,1)} %param.15) | copy-start | bytes 6291460
  7.2 144.3 %all-reduce.7.cloned.1.call-start = ((), (), s32[]{:S(2)}) async-start(), calls=%async_computation | async-start | bytes 2097152 | tf_op jit(solution)/shard_map/psum | solution.py:89
  8.8 14.2 %copy-start.29 = (s32[2]{0:T(128)S(1)}, s32[2]{0:T(128)}, u32[]{:S(2)}) copy-start(s32[2]{0:T(128)} %param.11) | copy-start | bytes 28
  8.9 83.8 %copy-start.6 = (bf16[2,256,1024]{2,1,0:T(8,128)(2,1)S(1)}, bf16[2,256,1024]{2,1,0:T(8,128)(2,1)}, u32[]{:S(2)}) copy-start(bf16[2,256,1024]{2,1,0:T(8,128)(2,1)} %param.9) | copy-start | bytes 3145732
  22.9 70.4 %copy-start.30 = (f32[1024]{0:T(1024)S(1)}, f32[1024]{0:T(1024)}, u32[]{:S(2)}) copy-start(f32[1024]{0:T(1024)} %param.12) | copy-start | bytes 12292
  23.0 373.3 %all-reduce.9.cloned.1.call-start = ((), (), s32[]{:S(2)}) async-start(), calls=%async_computation.1 | async-start | bytes 27525120 | tf_op jit(solution)/shard_map/psum | solution.py:101
  92.7 2.6 copy-start.18
  97.6 2.0 copy-start.4
  99.8 1.4 copy-start.11
  104.2 1.9 copy-start.31
  104.2 1.9 copy-start.32
  124.2 1.3 copy-start.2
  124.6 1.9 copy-start.22
  125.5 2.5 copy-start.21
  133.8 1.7 copy-start.20
  141.2 1.7 copy-start.19
  151.5 3.5 copy-start.10
  151.5 3.7 copy-start.8
  155.0 1.7 copy-start.23
  155.3 2.0 copy-start.3
  159.5 1.6 slice-start.1
  159.5 2.2 slice-start.2
  160.8 1.8 slice-start
  162.7 9.6 %copy-start.12 = (f32[2,256,1024]{2,1,0:T(8,128)S(1)}, f32[2,256,1024]{2,1,0:T(8,128)}, u32[]{:S(2)}) copy-start(f32[2,256,1024]{2,1,0:T(8,128)} %copy-done.11) | copy-start | bytes 6291460
  218.3 2.8 copy-start.5
  222.1 6.0 %copy-start.13 = (f32[512,1024]{1,0:T(8,128)}, f32[512,1024]{1,0:T(8,128)S(1)}, u32[]{:S(2)}) copy-start(f32[512,1024]{1,0:T(8,128)S(1)} %get-tuple-element.17) | copy-start | bytes 6291460
  222.1 6.0 %copy-start.15 = (f32[512,1024]{1,0:T(8,128)}, f32[512,1024]{1,0:T(8,128)S(1)}, u32[]{:S(2)}) copy-start(f32[512,1024]{1,0:T(8,128)S(1)} %get-tuple-element.18) | copy-start | bytes 6291460
  228.1 1.6 copy-start.14
  396.3 8.0 %copy-start.27 = (f32[31,1024]{1,0:T(8,128)S(1)}, f32[31,1024]{1,0:T(8,128)}, u32[]{:S(2)}) copy-start(f32[31,1024]{1,0:T(8,128)} %get-tuple-element.30) | copy-start | bytes 380932
  396.3 8.7 %copy-start.17 = (f32[1024,1024]{1,0:T(8,128)S(1)}, f32[1024,1024]{1,0:T(8,128)}, u32[]{:S(2)}) copy-start(f32[1024,1024]{1,0:T(8,128)} %get-tuple-element.31) | copy-start | bytes 12582916
  405.0 2.1 copy-start.26
  405.0 3.8 copy-start.1
  (6 other events, 6.0 us)
Sparse Core Ops, SparseCore 0:
  23.1 50.1 all-reduce.6
  228.3 167.9 all-reduce.8
where the time goes:
time: 419 us; the launch traced here: 416 us
  blocking collectives  132 us (32%)
  waiting for transfers between devices  97.3 us (23%)
  matrix products  67.2 us (16%)
  local copies, waits for them, and re-layouts  60.9 us (15%)
  other arithmetic  42.6 us (10%)
  between operations  15.5 us (4%)
    psum x1, waiting for transfers between devices, on_device(): lax.psum((gradients[0], gradients[1].astype(jnp.float32), gradients[2], g...  97.3 us
    psum x1, blocking collectives, on_device(): lax.psum(jnp.sum(lengths.astype(jnp.float32)), ('member', 'dp'))  69 us
    psum x1, blocking collectives, on_device(): lax.psum((gradients[0], gradients[1].astype(jnp.float32), gradients[2], g...  63.3 us
    conv_general_dilated x3, matrix products, lower_part(): lax.conv_general_dilated(gated, weight_depth[:, None, :], (1,), [(half_wi...  44.3 us
    unnamed x73, local copies, waits for them, and re-layouts  27.9 us
    conv_general_dilated x9, local copies, waits for them, and re-layouts, lower_part(): lax.conv_general_dilated(gated, weight_depth[:, None, :], (1,), [(half_wi...  14.6 us
    reduce_sum x1, other arithmetic, on_device(): jax.nn.log_softmax(teacher_logits.astype(jnp.float32), axis=-1)  14.1 us
    dot_general x3, matrix products, lower_part(): projected = jnp.dot(normed, weight_in, preferred_element_type=jnp.float32)  13.4 us
  transfers between devices with their start and end apart: 2, of which 1 were waited for; matrix products, arithmetic and copies ran while one was open for 13% of the time, Pallas kernels for 0%

commit v1 on v0

--- a/solution.py
+++ b/solution.py
@@ -99,15 +99,18 @@
     losses, pullback = jax.vjp(local_loss, weights)
     gradients = pullback(jnp.ones_like(losses))[0]
     totals = lax.psum(
-        (
-            gradients[0],
-            gradients[1].astype(jnp.float32),
-            gradients[2],
-            gradients[3].astype(jnp.float32),
-            gradients[4],
-            gradients[5].astype(jnp.float32),
+        lax.psum(
+            (
+                gradients[0],
+                gradients[1].astype(jnp.float32),
+                gradients[2],
+                gradients[3].astype(jnp.float32),
+                gradients[4],
+                gradients[5].astype(jnp.float32),
+            ),
+            "dp",
         ),
-        ("member", "dp"),
+        "member",
     )
     return (totals[0], totals[1], totals[2], totals[3], totals[4], totals[5], losses)
 

time: 419 us -> 1250 us (2.98)
  waiting for transfers between devices: 97.3 us -> 818 us
  blocking collectives: 132 us -> 244 us
    psum x1, waiting for transfers between devices: 97.3 us -> 674 us  [on_device(): lax.psum((gradients[0], gradients[1].astype(jnp.float32), gradients[2], g...]
    psum x0 -> x1, waiting for transfers between devices: none -> 144 us  [on_device(): lax.psum(lax.psum((gradients[0], gradients[1].astype(jnp.float32), gradie...]
    psum x1, blocking collectives: 63.3 us -> 170 us  [on_device(): lax.psum((gradients[0], gradients[1].astype(jnp.float32), gradients[2], g...]
  transfers between devices with their start and end apart: 2 -> 3, of which waited for: 1 -> 2; matrix products, arithmetic and copies ran while one was open for 13% -> 4% of each run, Pallas kernels for 0% -> 0%
where the time goes in v1:
time: 1250 us
  waiting for transfers between devices  818 us (65%)
  blocking collectives  244 us (20%)
  matrix products  67.2 us (5%)
  local copies, waits for them, and re-layouts  60.9 us (5%)
  other arithmetic  42.6 us (3%)
  between operations  15.2 us (1%)
    psum x1, waiting for transfers between devices, on_device(): lax.psum((gradients[0], gradients[1].astype(jnp.float32), gradients[2], g...  674 us
    psum x1, blocking collectives, on_device(): lax.psum((gradients[0], gradients[1].astype(jnp.float32), gradients[2], g...  170 us
    psum x1, waiting for transfers between devices, on_device(): lax.psum(lax.psum((gradients[0], gradients[1].astype(jnp.float32), gradie...  144 us
    psum x1, blocking collectives, on_device(): lax.psum(jnp.sum(lengths.astype(jnp.float32)), ('member', 'dp'))  69 us
    conv_general_dilated x3, matrix products, lower_part(): lax.conv_general_dilated(gated, weight_depth[:, None, :], (1,), [(half_wi...  44.3 us
    unnamed x73, local copies, waits for them, and re-layouts  27.9 us
  transfers between devices with their start and end apart: 3, of which 2 were waited for; matrix products, arithmetic and copies ran while one was open for 4% of the time, Pallas kernels for 0%

profile of v1, /device:TPU:1, one launch (start us, length us, event | category | flops | bytes accessed | tf_op | source)
XLA Modules:
  0.0 1248.3 jit_solution(15701344253762218985)
XLA Ops:
  8.9 14.1 %fusion.27 = f32[4,256,256]{2,1,0:T(8,128)} fusion(bf16[2,4,256,256]{3,2,1,0:T(8,128)(2,1)} %param.10, f32[2,4,256]{2,1,0:T(4,128)S(1)} %reduce_max.36), kind=kOutput, calls=%fused_computation.43 | output fusion | flops 2885887 | bytes 2105344 | tf_op jit(solution)/shard_map/jit(log_softmax)/reduce_sum | solution.py:88
  23.7 69.0 %psum.99 = f32[]{:T(128)} all-reduce(f32[]{:T(128)} %convert_reduce_fusion.1), channel_id=1, replica_groups=mesh['member'=2,'dp'=64] {'member','dp'}, use_global_device_ids=true, to_apply=%region_9.10 | all-reduce | flops 1 | bytes 8 | tf_op jit(solution)/shard_map/psum | solution.py:85
  95.2 2.4 fusion.73
  104.3 1.9 fusion.3
  106.1 11.0 multiply_convert_fusion
  117.2 1.7 copy.49
  118.9 2.7 reshape.152
  121.6 2.6 fusion.71
  128.1 2.9 copy.56
  130.9 2.9 reshape.165
  133.8 1.7 copy-done.20
  135.5 2.9 copy.50
  138.3 2.9 reshape.161
  142.9 2.9 copy.53
  145.8 3.0 reshape.163
  149.5 2.0 subtract_subtract_fusion
  152.8 2.1 fusion.70
  162.7 9.6 fusion.31
  172.2 27.8 %fusion.68 = f32[31,1,1024]{2,1,0:T(1,128)S(1)} fusion(f32[2,256,1024]{2,0,1:T(2,128)S(1)} %fusion.31, f32[2,256,1024]{2,1,0:T(8,128)S(1)} %copy-done.12), kind=kOutput, calls=%fused_computation.115 | convolution fusion | flops 189136896 | bytes 4321280 | tf_op jit(solution)/shard_map/transpose(jvp())/conv_general_dilated | solution.py:33
  201.3 3.3 fusion.35
  206.9 5.5 fusion.39
  212.4 2.9 copy.61
  215.2 3.1 reshape.159
  218.3 1.9 slice_multiply_fusion
  222.3 5.8 convert_convert_fusion
  228.2 674.1 %all-reduce.12.cloned.1.call-done = (f32[1024,2048]{1,0:T(8,128)}, f32[31,1024]{1,0:T(8,128)}, f32[1024,1024]{1,0:T(8,128)}, f32[1024,256]{1,0:T(8,128)}) async-done(((f32[1024,2048]{1,0:T(8,128)}, f32[31,1024]{1,0:T(8,128)}, f32[1024,1024]{1,0:T(8,128)}, f32[1024,256]{1,0:T(8,128)}), (f32[1024,2048]{1,0:T(8,128)}, f32[31,1024]{1,0:T(8,128)}, f32[1024,1024]{1,0:T(8,128)}, ...) | async-done | bytes 13758480 | tf_op jit(solution)/shard_map/psum | solution.py:102
  903.9 5.2 fusion.22
  909.1 170.3 %all-reduce.2 = (f32[1024]{0:T(1024)S(1)}, f32[1024]{0:T(1024)S(1)}) all-reduce(f32[1024]{0:T(1024)S(1)} %fusion.22, f32[1024]{0:T(1024)S(1)} %get-tuple-element.7), channel_id=1, replica_groups=mesh['member'=2,'dp'=64] {'dp'}, use_global_device_ids=true, to_apply=%region_18.19 | all-reduce | flops 2048 | bytes 16384 | tf_op jit(solution)/shard_map/psum | solution.py:102
  1079.4 5.0 all-reduce.4
  1085.1 143.9 %all-reduce.14.cloned.1.call-done = (f32[1024,2048]{1,0:T(8,128)}, f32[31,1024]{1,0:T(8,128)}, f32[1024,1024]{1,0:T(8,128)}, f32[1024,256]{1,0:T(8,128)}) async-done(((f32[1024,2048]{1,0:T(8,128)}, f32[31,1024]{1,0:T(8,128)}, f32[1024,1024]{1,0:T(8,128)}, f32[1024,256]{1,0:T(8,128)}), (f32[1024,2048]{1,0:T(8,128)}, f32[31,1024]{1,0:T(8,128)}, f32[1024,1024]{1,0:T(8,128)}, ...) | async-done | bytes 13758480 | tf_op jit(solution)/shard_map/psum | solution.py:101
  1229.0 8.0 copy.108
  1237.7 2.1 copy.110
  (123 shorter events, 36.2 us)
Async XLA Ops:
  7.2 114.4 %copy-start = (bf16[1024,1024]{1,0:T(8,128)(2,1)S(1)}, bf16[1024,1024]{1,0:T(8,128)(2,1)}, u32[]{:S(2)}) copy-start(bf16[1024,1024]{1,0:T(8,128)(2,1)} %param.15) | copy-start | bytes 6291460
  7.2 144.4 %all-reduce.10.cloned.1.call-start = ((), (), s32[]{:S(2)}) async-start(), calls=%async_computation | async-start | bytes 2097152 | tf_op jit(solution)/shard_map/psum | solution.py:89
  8.8 14.2 %copy-start.29 = (s32[2]{0:T(128)S(1)}, s32[2]{0:T(128)}, u32[]{:S(2)}) copy-start(s32[2]{0:T(128)} %param.11) | copy-start | bytes 28
  8.9 83.8 %copy-start.6 = (bf16[2,256,1024]{2,1,0:T(8,128)(2,1)S(1)}, bf16[2,256,1024]{2,1,0:T(8,128)(2,1)}, u32[]{:S(2)}) copy-start(bf16[2,256,1024]{2,1,0:T(8,128)(2,1)} %param.9) | copy-start | bytes 3145732
  22.9 70.4 %copy-start.30 = (f32[1024]{0:T(1024)S(1)}, f32[1024]{0:T(1024)}, u32[]{:S(2)}) copy-start(f32[1024]{0:T(1024)} %param.12) | copy-start | bytes 12292
  23.0 879.3 %all-reduce.12.cloned.1.call-start = ((), (), s32[]{:S(2)}) async-start(), calls=%async_computation.1 | async-start | bytes 27525120 | tf_op jit(solution)/shard_map/psum | solution.py:102
  92.7 2.6 copy-start.18
  97.6 2.0 copy-start.4
  99.8 1.4 copy-start.11
  104.2 1.9 copy-start.31
  104.2 1.9 copy-start.32
  124.6 1.9 copy-start.22
  125.5 2.5 copy-start.21
  133.8 1.7 copy-start.20
  141.2 1.7 copy-start.19
  151.5 3.5 copy-start.10
  151.5 3.7 copy-start.8
  155.0 1.7 copy-start.23
  155.3 2.0 copy-start.3
  159.5 1.6 slice-start.1
  159.5 2.2 slice-start.2
  160.8 1.8 slice-start
  162.7 9.6 copy-start.12
  218.3 2.8 copy-start.5
  222.1 6.0 copy-start.13
  222.1 6.0 copy-start.15
  228.2 1000.8 %all-reduce.14.cloned.1.call-start = ((), (), s32[]{:S(2)}) async-start(), calls=%async_computation.2 | async-start | bytes 27525120 | tf_op jit(solution)/shard_map/psum | solution.py:101
  902.3 1.6 copy-start.14
  1229.0 8.0 copy-start.27
  1229.0 8.7 copy-start.17
  1237.7 2.1 copy-start.26
  1237.7 3.8 copy-start.1
  (7 other events, 7.3 us)
Sparse Core Ops, SparseCore 0:
  23.1 50.1 all-reduce.9
  228.3 673.9 all-reduce.11
  905.5 323.4 all-reduce.13
